TPU v7x, 256 devices: a whole 4x4x8 slice. The times are simulated.
256 devices in a mesh: row: 32 (over y, x, core), col: 8 (over z).
Axes of the slice: x: 4, y: 4, z: 8, core: 2. Of those that a mesh axis runs over, the one named last changes fastest.
Arguments:
- features: bfloat16 [32768, 512], P(('row', 'col')), may hold values from -6 to 6
- tile_data: bfloat16 [256, 32, 2, 128, 128], P('row', 'col'), as said below
- tile_ids: int32 [256, 32, 2], P('row', 'col'), may hold values from 0 to 7, as said below
- tile_counts: int32 [256, 32], P('row', 'col'), may hold values from 0 to 2, as said below
- hist_tiles: bfloat16 [256, 8, 128, 128], P('row', 'col'), may hold values from -0.1875 to 0.1875
- hist_ids: int32 [256, 8], P('row', 'col'), may hold values from 0 to 31
- hist_cache: bfloat16 [4096, 512], P('col'), may hold values from -6 to 6
- first_weight: bfloat16 [512, 512], replicated, may hold values from -0.25 to 0.25
- second_weight: bfloat16 [512, 512], replicated, may hold values from -0.25 to 0.25
- grad_out: bfloat16 [32768, 512], P(('row', 'col')), may hold values from -6 to 6
Outputs:
- embedding: bfloat16 [32768, 512], P(('row', 'col'))
- grad_first: float32 [512, 512], replicated
- grad_second: float32 [512, 512], replicated
Inputs may be any that keep to these rules, and one draw needn't show every extreme that they name: tile_ids[p, j, t] is a tile column within panel j; slots t >= tile_counts[p, j] are padding and must be ignored; the used slots of a tile row and panel name distinct columns; the matrix that the tiles describe is symmetric. `tile_counts`: the count depends only on the block row of the tile row and on the panel. `tile_data`: padded slots hold arbitrary values.
All inputs are finite; a program needn't handle non-finite values.
Results may differ from a plain program's by a relative error of at most 0.018.
Values may be sent and summed in bfloat16 or wider, within the bound.
No kernel may reach another device: no remote copies, remote signals or barrier semaphores. Data moves between devices by JAX's collectives and lax.ppermute only.
A program may use at most 128 MiB of HBM per device.

v0:
```python
import math

import jax
import jax.numpy as jnp
from jax import lax
from jax.sharding import PartitionSpec as P


def spread(shard, axis, root):
    mine = lax.axis_index(axis) == root
    return lax.psum(jnp.where(mine, shard, jnp.zeros_like(shard)), axis)


def pick_tiles(panel_rows, tile_data, tile_ids, tile_counts):
    tile_rows = tile_ids.shape[0]
    slot_count = tile_ids.shape[1]
    tile_size = tile_data.shape[-1]
    blocks = panel_rows.reshape(tile_rows, tile_size, panel_rows.shape[1])
    picked = blocks[tile_ids]
    keep_mask = (jnp.arange(slot_count)[None, :] < tile_counts[:, None]).astype(tile_data.dtype)
    masked = tile_data * keep_mask[:, :, None, None]
    product = jnp.einsum("atij,atjf->aif", masked, picked, preferred_element_type=jnp.float32)
    return product.reshape(tile_rows * tile_size, panel_rows.shape[1])


def aggregate(source, tile_data, tile_ids, tile_counts):
    section_total = tile_data.shape[1]
    col_index = lax.axis_index("col")
    running = jnp.zeros(source.shape, jnp.float32)
    for section_num in range(section_total):
        panel_rows = spread(source, "row", col_index * section_total + section_num)
        running = running + pick_tiles(
            panel_rows,
            tile_data[:, section_num],
            tile_ids[:, section_num],
            tile_counts[:, section_num],
        )
    return running


def local(
    features,
    tile_data,
    tile_ids,
    tile_counts,
    hist_tiles,
    hist_ids,
    hist_cache,
    first_weight,
    second_weight,
    grad_out,
):
    share_rows = features.shape[0]
    node_count = share_rows * lax.axis_size("row") * lax.axis_size("col")
    norm_scale = 1.0 / math.sqrt(node_count)
    contract_rows = (((0,), (0,)), ((), ()))
    feat_panel = lax.all_gather(features, "col", axis=0, tiled=True)
    first_sum = aggregate(feat_panel, tile_data, tile_ids, tile_counts)
    first_agg = lax.psum_scatter(
        first_sum.astype(jnp.bfloat16), "col", scatter_dimension=0, tiled=True
    )
    first_pre = jnp.dot(first_agg, first_weight, preferred_element_type=jnp.float32)
    hidden_share = jax.nn.silu(first_pre).astype(jnp.bfloat16)
    hidden_panel = lax.all_gather(hidden_share, "col", axis=0, tiled=True)
    second_sum = aggregate(hidden_panel, tile_data, tile_ids, tile_counts)
    tile_size = hist_tiles.shape[-1]
    feat_width = hist_cache.shape[1]
    whole_cache = lax.all_gather(hist_cache, "col", axis=0, tiled=True)
    cache_blocks = whole_cache.reshape(-1, tile_size, feat_width)
    picked = cache_blocks[hist_ids]
    history = jnp.einsum("ahij,ahjf->aif", hist_tiles, picked, preferred_element_type=jnp.float32)
    second_sum = second_sum + history.reshape(second_sum.shape)
    second_agg = lax.psum_scatter(
        second_sum.astype(jnp.bfloat16), "col", scatter_dimension=0, tiled=True
    )
    embedding = jnp.dot(second_agg, second_weight, preferred_element_type=jnp.float32).astype(
        jnp.bfloat16
    )
    grad_agg = lax.dot_general(
        grad_out, second_weight, (((1,), (1,)), ((), ())), preferred_element_type=jnp.float32
    ).astype(jnp.bfloat16)
    second_term = (
        lax.dot_general(second_agg, grad_out, contract_rows, preferred_element_type=jnp.float32)
        * norm_scale
    )
    grad_second = lax.psum(second_term, ("row", "col"))
    grad_panel = lax.all_gather(grad_agg, "col", axis=0, tiled=True)
    back_sum = aggregate(grad_panel, tile_data, tile_ids, tile_counts)
    grad_hidden = lax.psum_scatter(
        back_sum.astype(jnp.bfloat16), "col", scatter_dimension=0, tiled=True
    )
    sigmoid_gate = jax.nn.sigmoid(first_pre)
    grad_pre = (
        grad_hidden.astype(jnp.float32) * sigmoid_gate * (1.0 + first_pre * (1.0 - sigmoid_gate))
    ).astype(jnp.bfloat16)
    first_term = (
        lax.dot_general(first_agg, grad_pre, contract_rows, preferred_element_type=jnp.float32)
        * norm_scale
    )
    grad_first = lax.psum(first_term, ("row", "col"))
    return (embedding, grad_first, grad_second)


def solution(mesh):
    placed = (
        P(("row", "col"), None),
        P("row", "col", None, None, None),
        P("row", "col", None),
        P("row", "col"),
        P("row", "col", None, None),
        P("row", "col"),
        P("col", None),
        P(),
        P(),
        P(("row", "col"), None),
    )
    return jax.shard_map(
        local,
        mesh=mesh,
        in_specs=placed,
        out_specs=(P(("row", "col"), None), P(), P()),
        check_vma=False,
    )
```

profile of v0, /device:TPU:2, one launch (start us, length us, event | category | flops | bytes accessed | tf_op | source)
XLA Modules:
  0.0 899.5 jit_solution(7173406365842705599)
XLA Ops:
  7.2 2.1 convolution_convert_fusion
  9.4 0.7 all-gather.5.cloned.1.call-update
  10.2 41.6 %all-gather.11.cloned.1.call-done = bf16[1024,512]{1,0:T(8,128)(2,1)} async-done(((bf16[128,512]{1,0:T(8,128)(2,1)}), bf16[1024,512]{1,0:T(8,128)(2,1)}) %all-gather.11.cloned.1.call-update) | async-done | bytes 1048592 | tf_op jit(solution)/shard_map/all_gather | solution.py:87
  51.8 38.6 %all-gather.5.cloned.1.call-done = bf16[1024,512]{1,0:T(8,128)(2,1)} async-done(((bf16[128,512]{1,0:T(8,128)(2,1)}), bf16[1024,512]{1,0:T(8,128)(2,1)}) %all-gather.5.cloned.1.call-update) | async-done | bytes 1048592 | tf_op jit(solution)/shard_map/all_gather | solution.py:57
  90.4 4.9 broadcast_select_fusion
  95.4 0.6 copy-done.14
  96.0 0.1 copy.17
  96.1 0.1 reshape.300
  96.2 0.1 copy.18
  96.3 0.1 reshape.308
  96.3 0.1 copy.19
  96.4 0.1 reshape.316
  96.5 0.1 copy.20
  96.6 0.1 reshape.324
  96.7 0.1 fusion.29
  96.8 0.1 fusion.30
  96.9 0.1 fusion.27
  97.0 118.1 %all-reduce.11.cloned.1.call-done = (bf16[8,128,512]{2,1,0:T(8,128)(2,1)}, bf16[8,128,512]{2,1,0:T(8,128)(2,1)}, bf16[8,128,512]{2,1,0:T(8,128)(2,1)}, bf16[8,128,512]{2,1,0:T(8,128)(2,1)}) async-done(((bf16[8,128,512]{2,1,0:T(8,128)(2,1)}, bf16[8,128,512]{2,1,0:T(8,128)(2,1)}, bf16[8,128,512]{2,1,0:T(8,128)(2,1)}, bf16[8,128,512]{2,1,0:T(8,128)(2,1)}), (bf16[8,128,512]{2,1,0:T(8,128)(2,1)}, ...) | async-done | bytes 4194320 | tf_op jit(solution)/shard_map/psum | solution.py:11
  215.1 3.2 gather_fusion
  218.3 3.4 gather_fusion.1
  221.8 3.6 fusion.5
  225.4 1.8 fusion.8
  227.2 3.3 gather_fusion.2
  230.5 3.5 fusion.11
  234.0 3.3 gather_fusion.3
  237.3 5.1 fusion.2
  242.4 39.5 %reduce-scatter.4.cloned.1.call-done = bf16[128,512]{1,0:T(8,128)(2,1)} async-done(((bf16[1024,512]{1,0:T(8,128)(2,1)}), bf16[128,512]{1,0:T(8,128)(2,1)}) %reduce-scatter.4.cloned.1.call-update) | async-done | bytes 131088 | tf_op jit(solution)/shard_map/reduce_scatter | solution.py:59
  281.9 1.8 multiply_convert_fusion.1
  283.8 0.5 all-gather.9.cloned.1.call-update
  284.4 36.8 %all-gather.7.cloned.1.call-done = bf16[1024,512]{1,0:T(8,128)(2,1)} async-done(((bf16[128,512]{1,0:T(8,128)(2,1)}), bf16[1024,512]{1,0:T(8,128)(2,1)}) %all-gather.7.cloned.1.call-update) | async-done | bytes 1048592 | tf_op jit(solution)/shard_map/all_gather | solution.py:64
  321.2 3.3 broadcast_select_fusion.10
  324.6 0.0 reduce-scatter.6.cloned.1.call-start
  324.6 0.6 copy-done.17
  325.2 50.8 %all-gather.9.cloned.1.call-done = bf16[4096,512]{1,0:T(8,128)(2,1)} async-done(((bf16[512,512]{1,0:T(8,128)(2,1)}), bf16[4096,512]{1,0:T(8,128)(2,1)}) %all-gather.9.cloned.1.call-update) | async-done | bytes 4194320 | tf_op jit(solution)/shard_map/all_gather | solution.py:68
  376.0 3.8 gather_fusion.8
  379.8 130.5 %all-reduce.9.cloned.1.call-done = (bf16[8,128,512]{2,1,0:T(8,128)(2,1)}, bf16[8,128,512]{2,1,0:T(8,128)(2,1)}, bf16[8,128,512]{2,1,0:T(8,128)(2,1)}, bf16[8,128...) async-done(((bf16[8,128,512]{2,1,0:T(8,128)(2,1)}, ...) | async-done | bytes 8388624 | tf_op jit(solution)/shard_map/psum | solution.py:11
  510.3 3.2 gather_fusion.4
  513.5 3.4 fusion.4
  517.0 3.3 gather_fusion.5
  520.2 3.4 fusion.7
  523.6 3.3 gather_fusion.6
  527.0 3.5 fusion.10
  530.4 3.3 gather_fusion.7
  533.7 2.2 fusion.12
  536.0 0.6 copy-done.8
  536.6 3.6 fusion.1
  540.3 3.3 gather_fusion.9
  543.6 3.2 gather_fusion.10
  546.8 3.3 gather_fusion.11
  550.1 3.3 gather_fusion.12
  553.4 2.2 fusion.3
  555.6 0.5 fusion.6
  556.1 1.1 copy-done.4
  557.2 0.5 fusion.9
  557.7 1.1 copy-done.6
  558.8 1.7 fusion
  560.6 19.0 %reduce-scatter.6.cloned.1.call-done = bf16[128,512]{1,0:T(8,128)(2,1)} async-done(((bf16[1024,512]{1,0:T(8,128)(2,1)}), bf16[128,512]{1,0:T(8,128)(2,1)}) %reduce-scatter.6.cloned.1.call-update) | async-done | bytes 131088 | tf_op jit(solution)/shard_map/reduce_scatter | solution.py:73
  579.5 2.2 convolution_multiply_fusion
  581.8 38.6 %reduce-scatter.8.cloned.1.call-done = bf16[128,512]{1,0:T(8,128)(2,1)} async-done(((bf16[1024,512]{1,0:T(8,128)(2,1)}), bf16[128,512]{1,0:T(8,128)(2,1)}) %reduce-scatter.8.cloned.1.call-update) | async-done | bytes 131088 | tf_op jit(solution)/shard_map/reduce_scatter | solution.py:89
  620.3 2.3 convolution_multiply_fusion.1
  622.6 0.9 convolution_convert_fusion.1
  623.5 265.8 %all-reduce.7.cloned.1.call-done = (f32[512,512]{1,0:T(8,128)}, f32[512,512]{1,0:T(8,128)}) async-done(((f32[512,512]{1,0:T(8,128)}, f32[512,512]{1,0:T(8,128)}), (f32[512,512]{1,0:T(8,128)}, f32[512,512]{1,0:T(8,128)})) %all-reduce.7.cloned.1.call-update) | async-done | bytes 2097168 | tf_op jit(solution)/shard_map/psum | solution.py:100
  889.3 2.4 copy.47
  891.7 1.0 copy.48
  (56 shorter events, 0.6 us)
Async XLA Ops:
  7.2 274.7 %copy-start = (bf16[512,512]{1,0:T(8,128)(2,1)S(1)}, bf16[512,512]{1,0:T(8,128)(2,1)}, u32[]{:S(2)}) copy-start(bf16[512,512]{1,0:T(8,128)(2,1)} %param.17) | copy-start | bytes 1572868
  7.2 44.6 %all-gather.11.cloned.1.call-start = ((), (), s32[]{:S(2)}) async-start(), calls=%async_computation.8 | async-start | bytes 1179648 | tf_op jit(solution)/shard_map/all_gather | solution.py:87
  9.4 81.0 %all-gather.5.cloned.1.call-start = ((), (), s32[]{:S(2)}) async-start(), calls=%async_computation.3 | async-start | bytes 1179648 | tf_op jit(solution)/shard_map/all_gather | solution.py:57
  10.1 205.0 %all-reduce.11.cloned.1.call-start = ((), (), s32[]{:S(2)}) async-start(), calls=%async_computation.12 | async-start | bytes 8388608 | tf_op jit(solution)/shard_map/psum | solution.py:11
  95.3 0.7 copy-start.14
  95.3 1.4 copy-start.15
  95.3 186.6 %reduce-scatter.4.cloned.1.call-start = ((), (), s32[]{:S(2)}) async-start(), calls=%async_computation.4 | async-start | bytes 1179648 | tf_op jit(solution)/shard_map/reduce_scatter | solution.py:59
  218.3 3.4 copy-start.2
  221.8 3.6 copy-start.5
  242.4 78.8 %all-gather.7.cloned.1.call-start = ((), (), s32[]{:S(2)}) async-start(), calls=%async_computation.5 | async-start | bytes 1179648 | tf_op jit(solution)/shard_map/all_gather | solution.py:64
  283.8 92.3 %all-gather.9.cloned.1.call-start = ((), (), s32[]{:S(2)}) async-start(), calls=%async_computation.6 | async-start | bytes 4718592 | tf_op jit(solution)/shard_map/all_gather | solution.py:68
  284.3 225.9 %all-reduce.9.cloned.1.call-start = ((), (), s32[]{:S(2)}) async-start(), calls=%async_computation.11 | async-start | bytes 16777216 | tf_op jit(solution)/shard_map/psum | solution.py:11
  324.5 0.7 copy-start.17
  324.6 255.0 %reduce-scatter.6.cloned.1.call-start = ((), (), s32[]{:S(2)}) async-start(), calls=%async_computation.7 | async-start | bytes 1179648 | tf_op jit(solution)/shard_map/reduce_scatter | solution.py:73
  533.7 2.2 copy-start.7
  533.7 2.9 copy-start.8
  533.7 2.9 copy-start.13
  540.2 80.1 %reduce-scatter.8.cloned.1.call-start = ((), (), s32[]{:S(2)}) async-start(), calls=%async_computation.9 | async-start | bytes 1179648 | tf_op jit(solution)/shard_map/reduce_scatter | solution.py:89
  553.4 2.2 copy-start.3
  555.6 1.6 copy-start.4
  557.2 1.6 copy-start.6
  558.8 20.7 %copy-start.11 = (bf16[128,512]{1,0:T(8,128)(2,1)S(1)}, bf16[128,512]{1,0:T(8,128)(2,1)}, u32[]{:S(2)}) copy-start(bf16[128,512]{1,0:T(8,128)(2,1)} %param.19) | copy-start | bytes 393220
  560.5 59.8 %copy-start.16 = (bf16[128,512]{1,0:T(8,128)(2,1)S(1)}, bf16[128,512]{1,0:T(8,128)(2,1)}, u32[]{:S(2)}) copy-start(bf16[128,512]{1,0:T(8,128)(2,1)} %reduce-scatter.4.cloned.1.call-done) | copy-start | bytes 393220
  560.5 328.8 %all-reduce.7.cloned.1.call-start = ((), (), s32[]{:S(2)}) async-start(), calls=%async_computation.10 | async-start | bytes 4194304 | tf_op jit(solution)/shard_map/psum | solution.py:100
  581.8 40.8 %copy-start.9 = (bf16[512,512]{1,0:T(8,128)(2,1)S(1)}, bf16[512,512]{1,0:T(8,128)(2,1)}, u32[]{:S(2)}) copy-start(bf16[512,512]{1,0:T(8,128)(2,1)} %param.18) | copy-start | bytes 1572868
  581.8 40.9 %copy-start.12 = (bf16[128,512]{1,0:T(8,128)(2,1)S(1)}, bf16[128,512]{1,0:T(8,128)(2,1)}, u32[]{:S(2)}) copy-start(bf16[128,512]{1,0:T(8,128)(2,1)} %reduce-scatter.6.cloned.1.call-done) | copy-start | bytes 393220
  889.3 2.4 copy-start.10
  889.3 3.4 copy-start.1
Sparse Core Ops, SparseCore 0:
  10.3 41.3 all-gather.10
  53.5 36.7 all-gather.4
  95.5 119.5 all-reduce.10
  242.5 39.3 reduce-scatter.3
  284.1 37.0 all-gather.6
  322.9 53.1 all-gather.8
  380.7 129.5 all-reduce.8
  540.4 39.1 reduce-scatter.5
  582.7 37.6 reduce-scatter.7
  626.3 262.9 all-reduce.6
where the time goes:
time: 901 us; the launch traced here: 900 us
  waiting for transfers between devices  781 us (87%)
  local copies, waits for them, and re-layouts  51.3 us (6%)
  matrix products  44.3 us (5%)
  between operations  14.3 us (2%)
    psum x1, waiting for transfers between devices, local(): grad_first = lax.psum(first_term, ('row', 'col'))  266 us
    psum x2, waiting for transfers between devices, spread(): return lax.psum(jnp.where(mine, shard, jnp.zeros_like(shard)), axis)  249 us
    all_gather x1, waiting for transfers between devices, local(): whole_cache = lax.all_gather(hist_cache, 'col', axis=0, tiled=True)  50.8 us
    all_gather x1, waiting for transfers between devices, local(): grad_panel = lax.all_gather(grad_agg, 'col', axis=0, tiled=True)  41.6 us
    gather x12, local copies, waits for them, and re-layouts, pick_tiles(): picked = blocks[tile_ids]  39.5 us
    reduce_scatter x1, waiting for transfers between devices, local(): lax.psum_scatter(first_sum.astype(jnp.bfloat16), 'col', scatter_dimension...  39.5 us
    all_gather x1, waiting for transfers between devices, local(): feat_panel = lax.all_gather(features, 'col', axis=0, tiled=True)  38.6 us
    reduce_scatter x1, waiting for transfers between devices, local(): lax.psum_scatter(back_sum.astype(jnp.bfloat16), 'col', scatter_dimension=...  38.6 us
  transfers between devices with their start and end apart: 10, of which 10 were waited for; matrix products, arithmetic and copies ran while one was open for 3% of the time, Pallas kernels for 0%

commit v1 on v0

v1 whole, which is shorter than its diff:
```python
import functools
import math

import jax
import jax.numpy as jnp
from jax import lax
from jax.experimental import pallas as pl
from jax.experimental.pallas import tpu as pltpu
from jax.sharding import Mesh, PartitionSpec as P

BF = jnp.bfloat16
F32 = jnp.float32
TILE = 128
VMEM = pl.BlockSpec(memory_space=pltpu.VMEM)
SMEM = pl.BlockSpec(memory_space=pltpu.SMEM)
ROWS = (((0,), (0,)), ((), ()))


def back_kernel(ids, counts, tiles, source, out, total):
    rows, panels, slots = tiles.shape[:3]
    width = total.shape[0] // panels // TILE
    total[...] = jnp.zeros_like(total)

    def one_row(p, carry):
        block = source[pl.ds(pl.multiple_of(p * TILE, TILE), TILE), :]
        for j in range(panels):
            used = counts[p, j]
            for t in range(slots):

                @pl.when(t < used)
                def _():
                    column = j * width + ids[p, j, t]
                    at = pl.ds(pl.multiple_of(column * TILE, TILE), TILE)
                    total[at, :] += lax.dot_general(
                        tiles[p, j, t], block, ROWS, preferred_element_type=F32
                    )

        return carry

    lax.fori_loop(0, rows, one_row, 0)
    out[...] = total[...].astype(out.dtype)


def back_product(ids, counts, tiles, source):
    rows, panels, slots = tiles.shape[:3]
    height = panels * 8 * TILE
    width = source.shape[1]
    return pl.pallas_call(
        back_kernel,
        out_shape=jax.ShapeDtypeStruct((height, width), BF),
        in_specs=[SMEM, SMEM, VMEM, VMEM],
        out_specs=VMEM,
        scratch_shapes=[pltpu.VMEM((height, width), F32)],
        compiler_params=pltpu.CompilerParams(vmem_limit_bytes=40 << 20),
        cost_estimate=pl.CostEstimate(
            flops=2 * rows * panels * slots * TILE * TILE * width,
            bytes_accessed=12 << 20,
            transcendentals=0,
        ),
        name="back_product",
    )(ids, counts, tiles, source)


def row_kernel(base, ids, counts, tiles, source, out):
    rows = out.shape[0] // TILE
    panels, slots = tiles.shape[1:3]
    width = source.shape[0] // panels // TILE

    def one_row(i, carry):
        p = base[0] + i
        acc = jnp.zeros((TILE, out.shape[1]), F32)
        for j in range(panels):
            used = counts[p, j]
            for t in range(slots):
                tile = tiles[p, j, t]
                tile = jnp.where(t < used, tile, jnp.zeros_like(tile))
                at = pl.multiple_of((j * width + ids[p, j, t]) * TILE, TILE)
                acc += jnp.dot(tile, source[pl.ds(at, TILE), :], preferred_element_type=F32)
        out[pl.ds(pl.multiple_of(i * TILE, TILE), TILE), :] = acc.astype(out.dtype)
        return carry

    lax.fori_loop(0, rows, one_row, 0)


def row_product(base, ids, counts, tiles, source, rows, dtype):
    panels, slots = tiles.shape[1:3]
    width = source.shape[1]
    return pl.pallas_call(
        row_kernel,
        out_shape=jax.ShapeDtypeStruct((rows * TILE, width), dtype),
        in_specs=[SMEM, SMEM, SMEM, VMEM, VMEM],
        out_specs=VMEM,
        compiler_params=pltpu.CompilerParams(vmem_limit_bytes=40 << 20),
        cost_estimate=pl.CostEstimate(
            flops=2 * rows * panels * slots * TILE * TILE * width,
            bytes_accessed=6 << 20,
            transcendentals=0,
        ),
        name="row_product",
    )(base, ids, counts, tiles, source)


def hist_kernel(place, ids, tiles, cache, out):
    splits, rows = tiles.shape[:2]
    blocks = cache.shape[0] // TILE
    first = place[0] * blocks

    def one_row(p, carry):
        at = pl.ds(pl.multiple_of(p * TILE, TILE), TILE)
        out[at, :] = jnp.zeros((TILE, out.shape[1]), F32)
        for q in range(splits):
            block = ids[q, p] - first

            @pl.when((block >= 0) & (block < blocks))
            def _():
                part = cache[pl.ds(pl.multiple_of(block * TILE, TILE), TILE), :]
                out[at, :] += jnp.dot(tiles[q, p], part, preferred_element_type=F32)

        return carry

    lax.fori_loop(0, rows, one_row, 0)


def hist_product(place, ids, tiles, cache):
    splits, rows = tiles.shape[:2]
    width = cache.shape[1]
    return pl.pallas_call(
        hist_kernel,
        out_shape=jax.ShapeDtypeStruct((rows * TILE, width), F32),
        in_specs=[SMEM, SMEM, VMEM, VMEM],
        out_specs=VMEM,
        compiler_params=pltpu.CompilerParams(vmem_limit_bytes=40 << 20),
        cost_estimate=pl.CostEstimate(
            flops=2 * rows * splits * TILE * TILE * width,
            bytes_accessed=5 << 20,
            transcendentals=0,
        ),
        name="hist_product",
    )(place, ids, tiles, cache)


def local(
    sizes,
    features,
    tile_data,
    tile_ids,
    tile_counts,
    hist_tiles,
    hist_ids,
    hist_cache,
    first_weight,
    second_weight,
    grad_out,
):
    chips, depth, everyone = sizes
    share, width = features.shape
    node_count = share * everyone
    scale = 1.0 / math.sqrt(node_count)
    core = lax.axis_index("core")
    place = lax.axis_index("z").astype(jnp.int32)[None]

    both = jnp.concatenate([features, grad_out], axis=1)
    pair_rows = lax.all_gather(both, ("core", "z"), axis=0, tiled=True)
    tiles = lax.all_to_all(tile_data, "core", split_axis=1, concat_axis=0, tiled=True)
    numbers = jnp.concatenate([tile_ids, tile_counts[:, :, None]], axis=2)
    numbers = lax.all_to_all(numbers, "core", split_axis=1, concat_axis=0, tiled=True)
    ids, counts = numbers[:, :, :2], numbers[:, :, 2]

    link_tiles = lax.all_gather(hist_tiles[:, 0], "z", axis=0)
    link_ids = lax.all_gather(hist_ids[:, 0], "z", axis=0)

    back = back_product(ids, counts, tiles, pair_rows)
    back = back.reshape(chips, share, 2 * width)
    back = lax.all_to_all(back, ("y", "x"), split_axis=0, concat_axis=0, tiled=True)
    summed = jnp.sum(back.astype(F32), axis=0).astype(BF)
    first_agg, grad_sum = summed[:, :width], summed[:, width:]

    first_pre = jnp.dot(first_agg, first_weight, preferred_element_type=F32)
    hidden = jax.nn.silu(first_pre).astype(BF)
    hidden_pair = lax.all_gather(hidden, ("y", "x"), axis=0, tiled=True)

    grad_hidden = lax.dot_general(
        grad_sum, second_weight, (((1,), (1,)), ((), ())), preferred_element_type=F32
    )
    gate = jax.nn.sigmoid(first_pre)
    grad_pre = (grad_hidden * gate * (1.0 + first_pre * (1.0 - gate))).astype(BF)
    history = hist_product(place, link_ids, link_tiles, hist_cache)
    own_grad = lax.dynamic_slice(
        pair_rows, (core * (share * depth), width), (share * depth, width)
    )
    first_term = lax.dot_general(first_agg, grad_pre, ROWS, preferred_element_type=F32)
    second_term = lax.dot_general(hidden, grad_sum, ROWS, preferred_element_type=F32)
    second_term += lax.dot_general(history.astype(BF), own_grad, ROWS, preferred_element_type=F32)
    terms = jnp.concatenate([first_term, second_term], axis=1).astype(BF)
    terms = terms.reshape(width // 16, 16, 2 * width // 128, 128).transpose(0, 2, 1, 3)
    terms = terms.reshape(everyone, 16, 128)
    terms = lax.all_to_all(terms, ("y", "x", "core", "z"), split_axis=0, concat_axis=0, tiled=True)
    term = (jnp.sum(terms.astype(F32), axis=0) * scale).astype(BF)
    spread = lax.all_to_all(
        jnp.broadcast_to(term[None], (everyone, 16, 128)),
        ("y", "x", "core", "z"),
        split_axis=0,
        concat_axis=0,
        tiled=True,
    )
    grads = spread.reshape(width // 16, 2 * width // 128, 16, 128).transpose(0, 2, 1, 3)
    grads = grads.reshape(width, 2 * width).astype(F32)

    rows = tile_data.shape[0]
    other = ((1 - core) * rows).astype(jnp.int32)[None]
    mine = (core * rows).astype(jnp.int32)[None]
    sent = row_product(other, ids, counts, tiles, hidden_pair, rows, BF)
    taken = lax.ppermute(sent, "core", [(0, 1), (1, 0)])
    kept = row_product(mine, ids, counts, tiles, hidden_pair, rows, F32)
    part = (kept + taken.astype(F32) + history).astype(BF).reshape(depth, share, width)
    part = lax.all_to_all(part, "z", split_axis=0, concat_axis=0, tiled=True)
    second_agg = jnp.sum(part.astype(F32), axis=0).astype(BF)
    embedding = jnp.dot(second_agg, second_weight, preferred_element_type=F32).astype(BF)
    return (embedding, grads[:, :width], grads[:, width:])


def solution(mesh):
    devices = mesh.devices.reshape(4, 4, 2, 8)
    chip_mesh = Mesh(devices, ("y", "x", "core", "z"))
    row = ("y", "x", "core")
    everything = ("y", "x", "core", "z")
    placed = (
        P(everything, None),
        P(row, "z", None, None, None),
        P(row, "z", None),
        P(row, "z"),
        P(row, "z", None, None),
        P(row, "z"),
        P("z", None),
        P(),
        P(),
        P(everything, None),
    )
    return jax.shard_map(
        functools.partial(local, (16, 8, 256)),
        mesh=chip_mesh,
        in_specs=placed,
        out_specs=(P(everything, None), P(), P()),
        check_vma=False,
    )
```

time: 901 us -> 289 us (0.32)
  waiting for transfers between devices: 781 us -> 117 us
  blocking collectives: 0 us -> 49.7 us
  matrix products: 44.3 us -> 7.28 us
  starting transfers between devices: 0.41 us -> 31.8 us
  local copies, waits for them, and re-layouts: 51.3 us -> 25.7 us
  Pallas kernels: 0 us -> 24.1 us
    psum x3 -> x0, waiting for transfers between devices: 514 us -> none  [the longest x1 266 us: local(): grad_first = lax.psum(first_term, ('row', 'col'))]
    all_gather x4 -> x3, waiting for transfers between devices: 168 us -> 58 us  [the longest x1 29.2 us: local(): link_tiles = lax.all_gather(hist_tiles[:, 0], 'z', axis=0)]
    reduce_scatter x3 -> x0, waiting for transfers between devices: 97 us -> none  [the longest x1 39.5 us: local(): lax.psum_scatter(first_sum.astype(jnp.bfloat16), 'col', scatter_dimension...]
    all_to_all x0 -> x5, waiting for transfers between devices: none -> 58.2 us  [the longest x1 25.8 us: local(): part = lax.all_to_all(part, 'z', split_axis=0, concat_axis=0, tiled=True)]
    gather x13 -> x0, local copies, waits for them, and re-layouts: 43.3 us -> none  [the longest x12 39.5 us: pick_tiles(): picked = blocks[tile_ids]]
    all_to_all x0 -> x1, blocking collectives: none -> 39.5 us  [local(): lax.all_to_all(terms, ('y', 'x', 'core', 'z'), split_axis=0, concat_axis=...]
    dot_general x18 -> x5, matrix products: 44.3 us -> 7.28 us  [the longest x1 2.68 us: local(): lax.dot_general(history.astype(BF), own_grad, ROWS, preferred_element_typ...]
    all_to_all x0 -> x5, starting transfers between devices: none -> 31.5 us  [the longest x1 10.8 us: local(): lax.all_to_all(back, ('y', 'x'), split_axis=0, concat_axis=0, tiled=True)]
  transfers between devices with their start and end apart: 10 -> 9, of which waited for: 10 -> 6; matrix products, arithmetic and copies ran while one was open for 3% -> 9% of each run, Pallas kernels for 0% -> 3%
where the time goes in v1:
time: 289 us; the launch traced here: 285 us
  waiting for transfers between devices  117 us (40%)
  blocking collectives  49.7 us (17%)
  starting transfers between devices  31.8 us (11%)
  local copies, waits for them, and re-layouts  25.7 us (9%)
  Pallas kernels  24.1 us (8%)
  between operations  16.4 us (6%)
  other arithmetic  13.2 us (5%)
  matrix products  7.28 us (3%)
    all_to_all x1, blocking collectives, local(): lax.all_to_all(terms, ('y', 'x', 'core', 'z'), split_axis=0, concat_axis=...  39.5 us
    all_gather x1, waiting for transfers between devices, local(): link_tiles = lax.all_gather(hist_tiles[:, 0], 'z', axis=0)  29.2 us
    all_gather x1, waiting for transfers between devices, local(): pair_rows = lax.all_gather(both, ('core', 'z'), axis=0, tiled=True)  28.7 us
    all_to_all x1, waiting for transfers between devices, local(): part = lax.all_to_all(part, 'z', split_axis=0, concat_axis=0, tiled=True)  25.8 us
    unnamed x37, local copies, waits for them, and re-layouts  17.6 us
    all_to_all x1, waiting for transfers between devices, local(): lax.all_to_all(jnp.broadcast_to(term[None], (everyone, 16, 128)), ('y', '...  15.6 us
    pallas_call x1, Pallas kernels, back_product(): pl.pallas_call(back_kernel, out_shape=jax.ShapeDtypeStruct((height, width...  14.3 us
    all_to_all x1, waiting for transfers between devices, local(): lax.all_to_all(back, ('y', 'x'), split_axis=0, concat_axis=0, tiled=True)  14.3 us
  transfers between devices with their start and end apart: 9, of which 6 were waited for; matrix products, arithmetic and copies ran while one was open for 9% of the time, Pallas kernels for 3%

profile of v1, /device:TPU:2, one launch (start us, length us, event | category | flops | bytes accessed | tf_op | source)
XLA Modules:
  0.0 284.9 jit_solution(12726522593892136601)
XLA Ops:
  8.0 0.0 copy-start
  8.0 0.0 all-gather.6.cloned.1.call-start
  8.1 1.7 pad_maximum_fusion.1
  9.8 0.0 all-gather.6.cloned.1.call-update
  9.8 1.3 pad_add_fusion
  11.1 3.2 %all-to-all-start = ((s32[8,4,3]{0,2,1:T(4,128)}), s32[8,4,3]{0,2,1:T(4,128)S(1)}, u32[]{:S(2)}, u32[]{:S(2)}) async-start(s32[8,4,3]{0,2,1:T(4,128)} %pad_add_fusion), calls=%async_computation | async-start | bytes 16384 | tf_op jit(solution)/shard_map/all_to_all | solution.py:166
  14.4 3.2 %copy.46 = bf16[8,4,2,128,128]{4,3,2,0,1:T(8,128)(2,1)} copy(bf16[8,4,2,128,128]{4,3,2,1,0:T(8,128)(2,1)} %param.11) | data formatting | bytes 4194304 | tf_op args[1]
  17.6 0.0 all-to-all-done
  17.6 3.8 %all-to-all-start.1 = ((bf16[8,4,2,128,128]{4,3,2,0,1:T(8,128)(2,1)}), bf16[8,4,2,128,128]{4,3,2,0,1:T(8,128)(2,1)S(1)}, u32[]{:S(2)}, u32[]{:S(2)}) async-start(bf16[8,4,2,128,128]{4,3,2,0,1:T(8,128)(2,1)} %copy.46), calls=%async_computation.1 | async-start | bytes 4194304 | tf_op jit(solution)/shard_map/all_to_all | solution.py:164
  21.4 0.1 all_to_all.41
  21.5 0.1 copy.54.ids
  21.6 0.1 copy.49.counts
  21.6 2.6 all-to-all-done.1
  24.2 1.3 copy-done.9
  25.5 1.8 copy.47
  27.4 28.7 %all-gather.6.cloned.1.call-done.source = bf16[2048,1024]{1,0:T(8,128)(2,1)} async-done(((bf16[128,1024]{1,0:T(8,128)(2,1)}), bf16[2048,1024]{1,0:T(8,128)(2,1)}) %all-gather.6.cloned.1.call-update) | async-done | bytes 4194320 | tf_op jit(solution)/shard_map/all_gather | solution.py:163
  56.1 2.2 copy-done.6
  58.3 14.3 %back_product.1 = bf16[2048,1024]{1,0:T(8,128)(2,1)S(1)} custom-call(s32[16,2,2]{2,1,0:T(2,128)S(1)} %copy.54.ids, s32[16,2]{1,0:T(8,128)S(1)} %copy.49.counts, bf16[16,2,2,128,128]{4,3,2,1,0:T(8,128)(2,1)S(1)} %bitcast.45, bf16[2048,1024]{1,0:T(8,128)(2,1)S(1)} %copy-done.6), custom_call_target="tpu_custom_call" | custom-call | flops 2147483648 | bytes 12582912 | tf_op jit(solution)/shard_map/back_product/pallas_call | solution.py:48
  72.6 2.0 copy-done.3
  74.5 10.8 %all-to-all-start.2 = ((bf16[16,128,1024]{2,1,0:T(8,128)(2,1)}), bf16[16,128,1024]{2,1,0:T(8,128)(2,1)}, u32[]{:S(2)}, u32[]{:S(2)}) async-start(bf16[16,128,1024]{2,1,0:T(8,128)(2,1)} %bitcast.48), calls=%async_computation.2 | async-start | bytes 8388608 | tf_op jit(solution)/shard_map/all_to_all | solution.py:174
  85.3 0.0 all-gather.10.cloned.1.call-start
  85.3 0.5 all-gather.10.cloned.1.call-update
  85.9 0.0 all-gather.8.cloned.1.call-start
  85.9 0.6 dynamic-slice
  87.2 0.1 bitcast_dynamic-update-slice_fusion
  87.3 10.2 %all-reduce = s32[64]{0:T(128)S(1)} all-reduce(s32[64]{0:T(128)S(1)} %bitcast_dynamic-update-slice_fusion), channel_id=2, replica_groups=mesh['y'=4,'x'=4,'core'=2,'z'=8] {'z'}, use_global_device_ids=true, to_apply=%add | all-reduce | flops 64 | bytes 512
  97.5 0.1 reshape.33.ids
  97.6 29.2 %all-gather.10.cloned.1.call-done = bf16[64,1,128,128]{3,2,1,0:T(8,128)(2,1)} async-done(((bf16[8,1,128,128]{3,2,1,0:T(8,128)(2,1)}), bf16[64,1,128,128]{3,2,1,0:T(8,128)(2,1)}) %all-gather.10.cloned.1.call-update) | async-done | bytes 2097168 | tf_op jit(solution)/shard_map/all_gather | solution.py:169
  126.8 1.6 copy-done.7
  128.4 2.4 hist_product.1
  130.8 1.3 copy-done.1
  132.1 14.3 %all-to-all-done.2 = bf16[16,128,1024]{2,1,0:T(8,128)(2,1)} async-done(((bf16[16,128,1024]{2,1,0:T(8,128)(2,1)}), bf16[16,128,1024]{2,1,0:T(8,128)(2,1)}, u32[]{:S(2)}, u32[]{:S(2)}) %all-to-all-start.2) | async-done | bytes 4194336 | tf_op jit(solution)/shard_map/all_to_all | solution.py:174
  146.3 3.1 %reduce_sum.33 = bf16[128,1024]{1,0:T(8,128)(2,1)S(1)} reduce(bf16[16,128,1024]{2,1,0:T(8,128)(2,1)} %all-to-all-done.2, bf16[]{:T(256)} %constant.9.clone.1), dimensions={0}, to_apply=%region_0.0 | reduce | flops 1966080 | bytes 4456450 | tf_op jit(solution)/shard_map/reduce_sum | solution.py:175
  149.5 1.0 multiply_convert_fusion
  150.5 0.0 all-gather.8.cloned.1.call-update
  150.5 2.4 convolution_convert_fusion
  152.9 0.3 fusion.9
  153.2 0.0 copy-start.11
  153.2 2.7 fusion
  155.9 1.0 pad_maximum_fusion
  157.0 2.3 copy.51
  159.2 1.5 copy.55
  160.7 0.1 bitcast_bitcast_fusion
  160.8 0.2 copy.52
  161.1 39.5 %all_to_all.56 = bf16[256,16,128]{2,1,0:T(8,128)(2,1)S(1)} all-to-all(bf16[256,16,128]{2,1,0:T(8,128)(2,1)S(1)} %bitcast.55), channel_id=1, replica_groups=mesh['y'=4,'x'=4,'core'=2,'z'=8] {'y','x','core','z'}, dimensions={0} | all-to-all | bytes 2097152 | tf_op jit(solution)/shard_map/all_to_all | solution.py:197
  200.6 0.3 convert_reduce_fusion
  200.9 1.1 broadcast_in_dim.22
  202.0 9.5 %all-to-all-start.5 = ((bf16[256,16,128]{2,1,0:T(8,128)(2,1)}), bf16[256,16,128]{2,1,0:T(8,128)(2,1)}, u32[]{:S(2)}, u32[]{:S(2)}) async-start(bf16[256,16,128]{2,1,0:T(8,128)(2,1)} %broadcast_in_dim.22), calls=%async_computation.5 | async-start | bytes 2097152 | tf_op jit(solution)/shard_map/all_to_all | solution.py:199
  211.5 0.0 all-gather.8.cloned.1.call-done.source
  211.6 1.6 copy-done.4
  213.1 4.2 %row_product.3 = bf16[1024,512]{1,0:T(8,128)(2,1)} custom-call(s32[1]{0:T(128)} %bitcast.11.base, s32[16,2,2]{2,1,0:T(2,128)S(1)} %copy.54.ids, s32[16,2]{1,0:T(8,128)S(1)} %copy.49.counts, bf16[16,2,2,128,128]{4,3,2,1,0:T(8,128)(2,1)S(1)} %bitcast.46, bf16[2048,512]{1,0:T(8,128)(2,1)S(1)} %copy-done.4), custom_call_target="tpu_custom_call" | custom-call | flops 536870912 | bytes 6291456 | tf_op jit(solution)/shard_map/row_product/pallas_call | solution.py:88
  217.3 0.1 collective-permute-start
  217.5 1.6 copy-done.5
  219.1 3.2 %row_product.2 = f32[1024,512]{1,0:T(8,128)S(1)} custom-call(s32[1]{0:T(128)} %bitcast.base, s32[16,2,2]{2,1,0:T(2,128)S(1)} %copy.54.ids, s32[16,2]{1,0:T(8,128)S(1)} %copy.49.counts, bf16[16,2,2,128,128]{4,3,2,1,0:T(8,128)(2,1)S(1)} %bitcast.47, bf16[2048,512]{1,0:T(8,128)(2,1)S(1)} %copy-done.5), custom_call_target="tpu_custom_call" | custom-call | flops 536870912 | bytes 6291456 | tf_op jit(solution)/shard_map/row_product/pallas_call | solution.py:88
  222.3 2.8 add_convert_fusion
  225.2 15.6 %all-to-all-done.5 = bf16[256,16,128]{2,1,0:T(8,128)(2,1)} async-done(((bf16[256,16,128]{2,1,0:T(8,128)(2,1)}), bf16[256,16,128]{2,1,0:T(8,128)(2,1)}, u32[]{:S(2)}, u32[]{:S(2)}) %all-to-all-start.5) | async-done | bytes 1048608 | tf_op jit(solution)/shard_map/all_to_all | solution.py:199
  240.8 4.2 %all-to-all-start.3 = ((bf16[8,128,512]{2,1,0:T(8,128)(2,1)}), bf16[8,128,512]{2,1,0:T(8,128)(2,1)}, u32[]{:S(2)}, u32[]{:S(2)}) async-start(bf16[8,128,512]{2,1,0:T(8,128)(2,1)} %bitcast.16), calls=%async_computation.3 | async-start | bytes 2097152 | tf_op jit(solution)/shard_map/all_to_all | solution.py:216
  245.0 1.5 convert_bitcast_fusion
  246.5 0.9 copy.53
  247.4 0.5 copy.58
  247.8 1.5 fusion.18
  249.3 25.8 %all-to-all-done.3 = bf16[8,128,512]{2,1,0:T(8,128)(2,1)} async-done(((bf16[8,128,512]{2,1,0:T(8,128)(2,1)}), bf16[8,128,512]{2,1,0:T(8,128)(2,1)}, u32[]{:S(2)}, u32[]{:S(2)}) %all-to-all-start.3) | async-done | bytes 1048608 | tf_op jit(solution)/shard_map/all_to_all | solution.py:216
  275.2 1.4 reduce_sum.34
  276.5 0.9 convolution_convert_fusion.1
  (28 shorter events, 0.1 us)
Async XLA Ops:
  8.0 142.5 %copy-start = (bf16[512,512]{1,0:T(8,128)(2,1)S(1)}, bf16[512,512]{1,0:T(8,128)(2,1)}, u32[]{:S(2)}) copy-start(bf16[512,512]{1,0:T(8,128)(2,1)} %param.18) | copy-start | bytes 1572868
  8.0 48.1 %all-gather.6.cloned.1.call-start = ((), (), s32[]{:S(2)}) async-start(), calls=%async_computation.6 | async-start | bytes 4456448 | tf_op jit(solution)/shard_map/all_gather | solution.py:163
  11.1 6.4 %all-to-all-start = ((s32[8,4,3]{0,2,1:T(4,128)}), s32[8,4,3]{0,2,1:T(4,128)S(1)}, u32[]{:S(2)}, u32[]{:S(2)}) async-start(s32[8,4,3]{0,2,1:T(4,128)} %pad_add_fusion), calls=%async_computation | async-start | bytes 16384 | tf_op jit(solution)/shard_map/all_to_all | solution.py:166
  17.6 6.6 %all-to-all-start.1 = ((bf16[8,4,2,128,128]{4,3,2,0,1:T(8,128)(2,1)}), bf16[8,4,2,128,128]{4,3,2,0,1:T(8,128)(2,1)S(1)}, u32[]{:S(2)}, u32[]{:S(2)}) async-start(bf16[8,4,2,128,128]{4,3,2,0,1:T(8,128)(2,1)} %copy.46), calls=%async_computation.1 | async-start | bytes 4194304 | tf_op jit(solution)/shard_map/all_to_all | solution.py:164
  24.2 1.3 copy-start.9
  56.1 2.2 copy-start.6
  72.6 2.0 copy-start.3
  74.5 11.4 %copy-start.14 = (u32[256]{0:T(256)S(1)}, u32[256]{0:T(256)}, u32[]{:S(2)}) copy-start(u32[256]{0:T(256)} %constant.41) | copy-start | bytes 3076
  74.5 12.7 %copy-start.13 = (s32[8,1]{0,1:T(1,128)S(1)}, s32[8,1]{0,1:T(1,128)}, u32[]{:S(2)}) copy-start(s32[8,1]{0,1:T(1,128)} %param.15) | copy-start | bytes 100
  74.5 52.2 %copy-start.8 = (bf16[512,512]{1,0:T(8,128)(2,1)S(1)}, bf16[512,512]{1,0:T(8,128)(2,1)}, u32[]{:S(2)}) copy-start(bf16[512,512]{1,0:T(8,128)(2,1)} %cache.1) | copy-start | bytes 1572868
  74.5 71.8 %all-to-all-start.2 = ((bf16[16,128,1024]{2,1,0:T(8,128)(2,1)}), bf16[16,128,1024]{2,1,0:T(8,128)(2,1)}, u32[]{:S(2)}, u32[]{:S(2)}) async-start(bf16[16,128,1024]{2,1,0:T(8,128)(2,1)} %bitcast.48), calls=%async_computation.2 | async-start | bytes 8388608 | tf_op jit(solution)/shard_map/all_to_all | solution.py:174
  85.3 41.5 %all-gather.10.cloned.1.call-start = ((), (), s32[]{:S(2)}) async-start(), calls=%async_computation.8 | async-start | bytes 2359296 | tf_op jit(solution)/shard_map/all_gather | solution.py:169
  85.9 125.7 %all-gather.8.cloned.1.call-start = ((), (), s32[]{:S(2)}) async-start(), calls=%async_computation.7 | async-start | bytes 2228224 | tf_op jit(solution)/shard_map/all_gather | solution.py:180
  126.8 1.6 copy-start.7
  130.8 1.3 copy-start.1
  132.1 17.4 %copy-start.12 = (bf16[512,512]{1,0:T(8,128)(2,1)S(1)}, bf16[512,512]{1,0:T(8,128)(2,1)}, u32[]{:S(2)}) copy-start(bf16[512,512]{1,0:T(8,128)(2,1)} %param.17) | copy-start | bytes 1572868
  150.4 2.4 copy-start.10
  153.2 2.7 copy-start.11
  202.0 38.8 %all-to-all-start.5 = ((bf16[256,16,128]{2,1,0:T(8,128)(2,1)}), bf16[256,16,128]{2,1,0:T(8,128)(2,1)}, u32[]{:S(2)}, u32[]{:S(2)}) async-start(bf16[256,16,128]{2,1,0:T(8,128)(2,1)} %broadcast_in_dim.22), calls=%async_computation.5 | async-start | bytes 2097152 | tf_op jit(solution)/shard_map/all_to_all | solution.py:199
  211.6 1.6 copy-start.4
  217.3 5.0 %collective-permute-start = (bf16[1024,512]{1,0:T(8,128)(2,1)}, bf16[1024,512]{1,0:T(8,128)(2,1)}, u32[]{:S(2)}, u32[]{:S(2)}) collective-permute-start(bf16[1024,512]{1,0:T(8,128)(2,1)} %row_product.3), channel_id=1, source_target_pairs={{0,8},{8,0},{1,9},{9,1},{2,10},{10,2},{3,11},{11,3},{4,12},{12,4},... | collective-permute-start | bytes 3145736 | tf_op jit(solution)/shard_map/ppermute | solution.py:213
  217.5 1.6 copy-start.5
  219.1 3.2 %copy-start.2 = (f32[1024,512]{1,0:T(8,128)S(1)}, f32[1024,512]{1,0:T(8,128)}, u32[]{:S(2)}) copy-start(f32[1024,512]{1,0:T(8,128)} %copy-done.1) | copy-start | bytes 6291460
  240.8 34.4 %all-to-all-start.3 = ((bf16[8,128,512]{2,1,0:T(8,128)(2,1)}), bf16[8,128,512]{2,1,0:T(8,128)(2,1)}, u32[]{:S(2)}, u32[]{:S(2)}) async-start(bf16[8,128,512]{2,1,0:T(8,128)(2,1)} %bitcast.16), calls=%async_computation.3 | async-start | bytes 2097152 | tf_op jit(solution)/shard_map/all_to_all | solution.py:216
Sparse Core Ops, SparseCore 0:
  11.2 44.8 all-gather.5
  150.6 50.3 all-gather.7
Sparse Core Ops, SparseCore 1:
  87.6 39.2 all-gather.9
